TPU v7x, 32 devices: a whole 2x2x4 slice. The times are simulated.
32 devices in a mesh: row: 8 (over y, x, core), col: 4 (over z).
Axes of the slice: x: 2, y: 2, z: 4, core: 2. Of those that a mesh axis runs over, the one named last changes fastest.
Arguments:
- panel_u: bfloat16 [2, 8, 1024, 160], P(None, 'row', 'col'), may hold values from -6 to 6
- panel_v: bfloat16 [2, 8, 1024, 160], P(None, 'row', 'col'), may hold values from -0.0625 to 0.0625
- panel_rank: int32 [2, 8], P(None, 'row'), may hold values from 32 to 160, as said below
- diag_inverse: bfloat16 [1024, 1024], P('col'), as said below
- tile_u: bfloat16 [2, 8, 4, 1024, 160], P(None, 'row', 'col'), may hold values from -6 to 6
- tile_v: bfloat16 [2, 8, 4, 1024, 160], P(None, 'row', 'col'), may hold values from -0.5 to 0.5
- tile_rank: int32 [2, 8, 4], P(None, 'row', 'col'), may hold values from 32 to 160, as said below
- sketch: bfloat16 [2, 8, 4, 1024, 160], P(None, 'row', 'col'), may hold values from -6 to 6
Outputs:
- new_u: float32 [2, 8, 4, 1024, 160], P(None, 'row', 'col')
- new_v: float32 [2, 8, 4, 1024, 160], P(None, 'row', 'col')
Inputs may be any that keep to these rules, and one draw needn't show every extreme that they name: `panel_rank`: some panel tile has rank 160. `tile_rank`: some trailing tile has rank 160. `diag_inverse`: lower triangular with diagonal entries of 1 to 2.
All inputs are finite; a program needn't handle non-finite values.
Results may differ from a plain program's by a relative error of at most 0.0037.
Values may be sent and summed in bfloat16 or wider, within the bound.
No kernel may reach another device: no remote copies, remote signals or barrier semaphores. Data moves between devices by JAX's collectives and lax.ppermute only.
A program may use at most 64 MiB of HBM per device.

v0:
```python
import math
import jax
import jax.numpy as jnp
from jax import lax
from jax.sharding import PartitionSpec as P


def spread(value, axis, source):
    kept = jnp.where(lax.axis_index(axis) == source, value, 0).astype(value.dtype)
    return lax.psum(kept, axis)


def recompress(old_u, old_v, row_u, row_s, col_u, col_s, omega, rank):
    high = lax.Precision.HIGHEST
    width = old_u.shape[1]
    keep_flag = jnp.arange(width, dtype=jnp.int32) < rank
    keep = keep_flag.astype(jnp.float32)
    keep_half = keep_flag.astype(jnp.bfloat16)
    ou_half = old_u * keep_half
    ov_half = old_v * keep_half
    om_half = omega * keep_half
    coupling = jnp.dot(row_s.T, col_s, preferred_element_type=jnp.float32)
    small_left = jnp.dot(ov_half.T, om_half, preferred_element_type=jnp.float32)
    small_right = jnp.dot(col_u.T, om_half, preferred_element_type=jnp.float32)
    ou = ou_half.astype(jnp.float32)
    ov = ov_half.astype(jnp.float32)
    ru = row_u.astype(jnp.float32)
    cu = col_u.astype(jnp.float32)
    sketched = jnp.dot(ou, small_left, precision=high)
    sketched = sketched - jnp.dot(
        ru, jnp.dot(coupling, small_right, precision=high), precision=high
    )
    gram = jnp.dot(sketched.T, sketched, precision=high) + jnp.diag(1.0 - keep)
    lower = jnp.linalg.cholesky(gram)
    basis = lax.linalg.triangular_solve(
        lower, sketched, left_side=False, lower=True, transpose_a=True
    )
    factor = math.sqrt(old_u.shape[0])
    right = jnp.dot(ov, jnp.dot(ou.T, basis, precision=high), precision=high)
    right = right - jnp.dot(
        cu,
        jnp.dot(coupling.T, jnp.dot(ru.T, basis, precision=high), precision=high),
        precision=high,
    )
    return (basis * factor, right / factor)


def on_device(panel_u, panel_v, panel_rank, diag_inverse, tile_u, tile_v, tile_rank, sketch):
    width = panel_u.shape[3]
    keep = (
        jnp.arange(width, dtype=jnp.int32)[None, None, None, :] < panel_rank[:, :, None, None]
    ).astype(jnp.bfloat16)
    full_u, full_v = (
        lax.all_gather(panel_u * keep, "col", axis=2, tiled=True),
        lax.all_gather(panel_v * keep, "col", axis=2, tiled=True),
    )
    inverse = lax.all_gather(diag_inverse, "col", axis=0, tiled=True)
    solved = jnp.einsum(
        "ab,tsbr->tsar", inverse, full_v, preferred_element_type=jnp.float32
    ).astype(jnp.bfloat16)
    col_count = lax.axis_size("col")
    col_place = lax.axis_index("col")
    results_u = []
    results_v = []
    for column in range(tile_u.shape[0]):
        source = column * col_count + col_place
        col_u, col_s = (spread(full_u[0, 0], "row", source), spread(solved[0, 0], "row", source))
        fresh_u, fresh_v = recompress(
            tile_u[column, 0, 0],
            tile_v[column, 0, 0],
            full_u[1, 0],
            solved[1, 0],
            col_u,
            col_s,
            sketch[column, 0, 0],
            tile_rank[column, 0, 0],
        )
        results_u.append(fresh_u)
        results_v.append(fresh_v)
    stacked_u = jnp.stack(results_u)[:, None, None]
    stacked_v = jnp.stack(results_v)[:, None, None]
    return (stacked_u, stacked_v)


def solution(mesh):
    placed = (
        P(None, "row", "col", None),
        P(None, "row", "col", None),
        P(None, "row"),
        P("col", None),
        P(None, "row", "col", None, None),
        P(None, "row", "col", None, None),
        P(None, "row", "col"),
        P(None, "row", "col", None, None),
    )
    return jax.shard_map(
        on_device,
        mesh=mesh,
        in_specs=placed,
        out_specs=(P(None, "row", "col", None, None), P(None, "row", "col", None, None)),
        check_vma=False,
    )
```

profile of v0, /device:TPU:0, one launch (start us, length us, event | category | flops | bytes accessed | tf_op | source)
XLA Modules:
  0.0 269.2 jit_solution(11368111475773620207)
XLA Ops:
  7.2 0.7 all-gather.2.cloned.1.call-update
  8.0 1.3 fusion.77
  9.3 0.6 fusion.71
  10.6 0.7 convert_subtract_fusion
  11.3 0.7 compare_convert_fusion
  12.0 1.1 bitcast_multiply_fusion.15
  13.1 1.4 fusion.24
  14.9 27.4 %all_gather.9 = bf16[2,1,1024,160]{2,3,0,1:T(8,128)(2,1)S(1)} all-gather(bf16[2,1,256,160]{2,3,0,1:T(8,128)(2,1)S(1)} %get-tuple-element.50), channel_id=1, replica_groups=mesh['row'=8,'col'=4] {'col'}, dimensions={2}, use_global_device_ids=true | all-gather | bytes 819200 | tf_op jit(solution)/shard_map/all_gather | solution.py:54
  42.3 26.6 %all_gather.10 = bf16[2,1,1024,160]{2,3,0,1:T(8,128)(2,1)S(1)} all-gather(bf16[2,1,256,160]{2,3,0,1:T(8,128)(2,1)S(1)} %get-tuple-element.51), channel_id=1, replica_groups=mesh['row'=8,'col'=4] {'col'}, dimensions={2}, use_global_device_ids=true | all-gather | bytes 819200 | tf_op jit(solution)/shard_map/all_gather | solution.py:55
  68.9 0.9 select_bitcast_fusion.2
  69.8 6.8 %all-gather.2.cloned.1.call-done = bf16[1024,1024]{1,0:T(8,128)(2,1)} async-done(((bf16[256,1024]{1,0:T(8,128)(2,1)}), bf16[1024,1024]{1,0:T(8,128)(2,1)}) %all-gather.2.cloned.1.call-update) | async-done | bytes 2097168 | tf_op jit(solution)/shard_map/all_gather | solution.py:57
  76.6 2.5 fusion.5
  79.1 0.9 select_bitcast_fusion.3
  81.2 1.5 fusion.45
  82.7 55.3 %all-reduce.6.cloned.1.call-done = (bf16[1024,160]{0,1:T(8,128)(2,1)}, bf16[1024,160]{0,1:T(8,128)(2,1)}, bf16[1024,160]{0,1:T(8,128)(2,1)}, bf16[1024,160]{0,1:T(8,128)(2,1)}) async-done(((bf16[1024,160]{0,1:T(8,128)(2,1)}, bf16[1024,160]{0,1:T(8,128)(2,1)}, bf16[1024,160]{0,1:T(8,128)(2,1)}, bf16[1024,160]{0,1:T(8,128)(2,1)}), (bf16[1024,160]{0,1:T(8,128)(2,1)}, bf16[1024,160]{0,1:T(8,128)(2,1)}, ...) | async-done | bytes 1310736 | tf_op jit(solution)/shard_map/psum | solution.py:10
  138.0 1.4 fusion.23
  139.4 1.2 fusion.35
  141.4 0.7 convolution_add_fusion
  142.3 11.7 %cholesky.174 = f32[128,128]{1,0:T(8,128)S(1)} custom-call(f32[128,128]{1,0:T(8,128)S(1)} %cholesky.211), custom_call_target="Cholesky" | custom-call | tf_op jit(solution)/shard_map/jit(cholesky)/cholesky | solution.py:34
  154.0 0.7 select_reduce_fusion
  154.7 1.4 fusion.27
  156.1 1.2 fusion.36
  158.1 0.7 convolution_add_fusion.1
  159.0 11.9 %cholesky.136 = f32[128,128]{1,0:T(8,128)S(1)} custom-call(f32[128,128]{1,0:T(8,128)S(1)} %cholesky.208), custom_call_target="Cholesky" | custom-call | tf_op jit(solution)/shard_map/jit(cholesky)/cholesky | solution.py:34
  170.9 10.6 %custom-call.15 = f32[1,128,128]{1,2,0:T(8,128)S(1)} custom-call(f32[1,128,128]{2,1,0:T(8,128)} %get-tuple-element.45), custom_call_target="InvertDiagBlocksLowerTriangular" | custom-call | tf_op jit(solution)/shard_map/jit(cholesky)/cholesky | solution.py:34
  181.9 2.9 %cholesky.194 = f32[32,32]{1,0:T(8,128)S(1)} custom-call(f32[32,32]{1,0:T(8,128)S(1)} %convolution_subtract_fusion.6), custom_call_target="Cholesky" | custom-call | tf_op jit(solution)/shard_map/jit(cholesky)/cholesky | solution.py:34
  184.8 0.6 compare_reduce_fusion
  185.5 0.6 compare_reduce_fusion.1
  187.4 0.6 copy-done.6
  188.1 9.8 %custom-call.13 = f32[1,128,128]{1,2,0:T(8,128)S(1)} custom-call(f32[1,128,128]{2,1,0:T(8,128)S(1)} %get-tuple-element.43), custom_call_target="InvertDiagBlocksLowerTriangular" | custom-call | tf_op jit(solution)/shard_map/jit(cholesky)/cholesky | solution.py:34
  198.2 2.9 %cholesky.156 = f32[32,32]{1,0:T(8,128)S(1)} custom-call(f32[32,32]{1,0:T(8,128)S(1)} %convolution_subtract_fusion.7), custom_call_target="Cholesky" | custom-call | tf_op jit(solution)/shard_map/jit(cholesky)/cholesky | solution.py:34
  201.8 0.6 compare_reduce_fusion.3
  203.6 0.7 select_select_fusion.1
  204.3 0.7 slice.139
  205.0 0.8 slice_bitcast_fusion.13
  206.0 0.7 pad_maximum_fusion.6
  206.6 19.7 %custom-call.14 = f32[2,128,128]{1,2,0:T(8,128)S(1)} custom-call(f32[2,128,128]{2,1,0:T(8,128)S(1)} %get-tuple-element.58), custom_call_target="InvertDiagBlocksLowerTriangular" | custom-call | tf_op jit(solution)/shard_map/triangular_solve/custom-call.0 | solution.py:35
  226.3 0.6 copy-done.10
  227.6 1.2 convolution_subtract_fusion.5
  228.8 1.0 fusion.68
  230.3 1.2 fusion.20
  231.5 20.5 %custom-call.16 = f32[2,128,128]{1,2,0:T(8,128)S(1)} custom-call(f32[2,128,128]{2,1,0:T(8,128)} %get-tuple-element.59), custom_call_target="InvertDiagBlocksLowerTriangular" | custom-call | tf_op jit(solution)/shard_map/triangular_solve/custom-call.0 | solution.py:35
  252.0 0.6 copy-done.11
  252.6 0.6 fusion.13
  253.3 1.1 convolution_subtract_fusion.4
  254.4 1.0 fusion.65
  260.1 1.1 maximum_bitcast_fusion.1
  261.2 1.2 maximum_bitcast_fusion
  (68 shorter events, 11.1 us)
Async XLA Ops:
  7.2 7.3 %copy-start.12 = (bf16[2,1,1,1024,160]{3,4,2,1,0:T(8,128)(2,1)S(1)}, bf16[2,1,1,1024,160]{3,4,2,1,0:T(8,128)(2,1)}, u32[]{:S(2)}) copy-start(bf16[2,1,1,1024,160]{3,4,2,1,0:T(8,128)(2,1)} %param.18) | copy-start | bytes 1966084
  7.2 7.3 %copy-start.4 = (bf16[2,1,1,1024,160]{3,4,2,1,0:T(8,128)(2,1)S(1)}, bf16[2,1,1,1024,160]{3,4,2,1,0:T(8,128)(2,1)}, u32[]{:S(2)}) copy-start(bf16[2,1,1,1024,160]{3,4,2,1,0:T(8,128)(2,1)} %param.16) | copy-start | bytes 1966084
  7.2 69.5 %all-gather.2.cloned.1.call-start = ((), (), s32[]{:S(2)}) async-start(), calls=%async_computation | async-start | bytes 2621440 | tf_op jit(solution)/shard_map/all_gather | solution.py:57
  7.9 130.1 %all-reduce.6.cloned.1.call-start = ((), (), s32[]{:S(2)}) async-start(), calls=%async_computation.1 | async-start | bytes 2621440 | tf_op jit(solution)/shard_map/psum | solution.py:10
  79.1 60.3 %copy-start = (bf16[2,1,1024,160]{2,3,0,1:T(8,128)(2,1)}, bf16[2,1,1024,160]{2,3,0,1:T(8,128)(2,1)S(1)}, u32[]{:S(2)}) copy-start(bf16[2,1,1024,160]{2,3,0,1:T(8,128)(2,1)S(1)} %fusion.5) | copy-start | bytes 1966084
  79.1 1.6 copy-start.2
  142.1 14.0 %copy-start.1 = (bf16[2,1,1024,160]{2,3,0,1:T(8,128)(2,1)S(1)}, bf16[2,1,1024,160]{2,3,0,1:T(8,128)(2,1)}, u32[]{:S(2)}) copy-start(bf16[2,1,1024,160]{2,3,0,1:T(8,128)(2,1)} %copy-done) | copy-start | bytes 1966084
  187.4 0.7 copy-start.6
  226.3 0.7 copy-start.10
  227.6 2.7 %copy-start.3 = (bf16[2,1,1,1024,160]{3,4,2,1,0:T(8,128)(2,1)S(1)}, bf16[2,1,1,1024,160]{3,4,2,1,0:T(8,128)(2,1)}, u32[]{:S(2)}) copy-start(bf16[2,1,1,1024,160]{3,4,2,1,0:T(8,128)(2,1)} %param.15) | copy-start | bytes 1966084
  252.0 0.7 copy-start.11
  256.4 1.1 copy-start.5
  256.4 1.1 copy-start.9
  257.5 1.6 copy-start.8
  258.6 1.0 copy-start.7
Sparse Core Ops, SparseCore 0:
  9.6 67.0 all-gather.1
  80.6 57.3 all-reduce.5
where the time goes:
time: 270 us; the launch traced here: 269 us
  other arithmetic  103 us (38%)
  waiting for transfers between devices  62.8 us (23%)
  blocking collectives  54 us (20%)
  matrix products  26.2 us (10%)
  between operations  17.2 us (6%)
  local copies, waits for them, and re-layouts  5.59 us (2%)
    psum x1, waiting for transfers between devices, spread(): return lax.psum(kept, axis)  55.3 us
    another operation x14, other arithmetic, recompress(): lower = jnp.linalg.cholesky(gram)  53.1 us
    another operation x8, other arithmetic, recompress(): lax.linalg.triangular_solve(lower, sketched, left_side=False, lower=True,...  41.6 us
    all_gather x1, blocking collectives, on_device(): lax.all_gather(panel_u * keep, 'col', axis=2, tiled=True)  27.4 us
    all_gather x1, blocking collectives, on_device(): lax.all_gather(panel_v * keep, 'col', axis=2, tiled=True)  26.6 us
    all_gather x1, waiting for transfers between devices, on_device(): inverse = lax.all_gather(diag_inverse, 'col', axis=0, tiled=True)  6.83 us
    another operation x6, matrix products, recompress(): lax.linalg.triangular_solve(lower, sketched, left_side=False, lower=True,...  5.61 us
  transfers between devices with their start and end apart: 2, of which 2 were waited for; matrix products, arithmetic and copies ran while one was open for 4% of the time, Pallas kernels for 0%

commit v1 on v0

--- a/solution.py
+++ b/solution.py
@@ -51,7 +51,9 @@
         jnp.arange(width, dtype=jnp.int32)[None, None, None, :] < panel_rank[:, :, None, None]
     ).astype(jnp.bfloat16)
     full_u, full_v = (
-        lax.all_gather(panel_u * keep, "col", axis=2, tiled=True),
+        jnp.concatenate(
+            lax.all_to_all(jnp.stack([panel_u * keep] * lax.axis_size("col")), "col", 0, 0), axis=2
+        ),
         lax.all_gather(panel_v * keep, "col", axis=2, tiled=True),
     )
     inverse = lax.all_gather(diag_inverse, "col", axis=0, tiled=True)

time: 270 us -> 265 us (0.981)
  starting transfers between devices: 0.08 us -> 6.39 us
  matrix products: 26.2 us -> 20.8 us
  blocking collectives: 54 us -> 49.3 us
    all_gather x1 -> x0, blocking collectives: 27.4 us -> none  [on_device(): lax.all_gather(panel_u * keep, 'col', axis=2, tiled=True)]
    all_gather x1, blocking collectives: 26.6 us -> 49.3 us  [on_device(): lax.all_gather(panel_v * keep, 'col', axis=2, tiled=True)]
    all_to_all x0 -> x1, starting transfers between devices: none -> 6.35 us  [on_device(): lax.all_to_all(jnp.stack([panel_u * keep] * lax.axis_size('col')), 'col',...]
    another operation x6, matrix products: 5.61 us -> 2.68 us  [recompress(): lax.linalg.triangular_solve(lower, sketched, left_side=False, lower=True,...]
  transfers between devices with their start and end apart: 2 -> 3, of which waited for: 2 -> 2; matrix products, arithmetic and copies ran while one was open for 4% -> 4% of each run, Pallas kernels for 0% -> 0%
where the time goes in v1:
time: 265 us
  other arithmetic  102 us (38%)
  waiting for transfers between devices  63.7 us (24%)
  blocking collectives  49.3 us (19%)
  matrix products  20.8 us (8%)
  between operations  17.2 us (6%)
  starting transfers between devices  6.39 us (2%)
  local copies, waits for them, and re-layouts  5.57 us (2%)
    psum x1, waiting for transfers between devices, spread(): return lax.psum(kept, axis)  55.7 us
    another operation x14, other arithmetic, recompress(): lower = jnp.linalg.cholesky(gram)  53.2 us
    all_gather x1, blocking collectives, on_device(): lax.all_gather(panel_v * keep, 'col', axis=2, tiled=True)  49.3 us
    another operation x8, other arithmetic, recompress(): lax.linalg.triangular_solve(lower, sketched, left_side=False, lower=True,...  41 us
    all_gather x1, waiting for transfers between devices, on_device(): inverse = lax.all_gather(diag_inverse, 'col', axis=0, tiled=True)  7.27 us
    all_to_all x1, starting transfers between devices, on_device(): lax.all_to_all(jnp.stack([panel_u * keep] * lax.axis_size('col')), 'col',...  6.35 us
  transfers between devices with their start and end apart: 3, of which 2 were waited for; matrix products, arithmetic and copies ran while one was open for 4% of the time, Pallas kernels for 0%

profile of v1, /device:TPU:0, one launch (start us, length us, event | category | flops | bytes accessed | tf_op | source)
XLA Modules:
  0.0 264.8 jit_solution(15636465008803923956)
XLA Ops:
  7.2 0.7 all-gather.2.cloned.1.call-update
  7.9 0.7 compare_convert_fusion
  8.6 1.2 bitcast_multiply_fusion.14
  9.8 0.9 stack.25
  10.7 6.3 %all-to-all-start = ((bf16[4,2,1,256,160]{3,4,2,1,0:T(8,128)(2,1)}), bf16[4,2,1,256,160]{3,4,2,1,0:T(8,128)(2,1)S(1)}, u32[]{:S(2)}, u32[]{:S(2)}) async-start(bf16[4,2,1,256,160]{3,4,2,1,0:T(8,128)(2,1)} %stack.25), calls=%async_computation | async-start | bytes 1310720 | tf_op jit(solution)/shard_map/all_to_all | solution.py:55
  17.1 0.6 fusion.78
  17.7 0.6 fusion.72
  18.3 0.6 fusion.73
  18.9 0.7 convert_subtract_fusion
  20.3 49.3 %all_gather.6 = bf16[2,1,1024,160]{2,3,0,1:T(8,128)(2,1)S(1)} all-gather(bf16[2,1,256,160]{2,3,0,1:T(8,128)(2,1)S(1)} %get-tuple-element.55), channel_id=1, replica_groups=mesh['row'=8,'col'=4] {'col'}, dimensions={2}, use_global_device_ids=true | all-gather | bytes 819200 | tf_op jit(solution)/shard_map/all_gather | solution.py:57
  69.9 0.8 copy.41
  70.9 0.8 copy.42
  71.7 7.3 %all-gather.2.cloned.1.call-done = bf16[1024,1024]{1,0:T(8,128)(2,1)} async-done(((bf16[256,1024]{1,0:T(8,128)(2,1)}), bf16[1024,1024]{1,0:T(8,128)(2,1)}) %all-gather.2.cloned.1.call-update) | async-done | bytes 2097168 | tf_op jit(solution)/shard_map/all_gather | solution.py:59
  79.0 2.5 fusion.5
  81.4 0.9 select_bitcast_fusion.1
  82.3 0.6 convert_subtract_fusion.1
  82.9 0.5 fusion.46
  83.5 0.5 fusion.45
  84.3 55.7 %all-reduce.6.cloned.1.call-done = (bf16[1024,160]{0,1:T(8,128)(2,1)}, bf16[1024,160]{0,1:T(8,128)(2,1)}, bf16[1024,160]{0,1:T(8,128)(2,1)}, bf16[1024,160]{0,1:T(8,128)(2,1)}) async-done(((bf16[1024,160]{0,1:T(8,128)(2,1)}, bf16[1024,160]{0,1:T(8,128)(2,1)}, bf16[1024,160]{0,1:T(8,128)(2,1)}, bf16[1024,160]{0,1:T(8,128)(2,1)}), (bf16[1024,160]{0,1:T(8,128)(2,1)}, bf16[1024,160]{0,1:T(8,128)(2,1)}, ...) | async-done | bytes 1310736 | tf_op jit(solution)/shard_map/psum | solution.py:10
  140.0 1.3 fusion.23
  141.3 1.2 fusion.35
  143.4 0.7 convolution_add_fusion
  144.3 11.7 %cholesky.174 = f32[128,128]{1,0:T(8,128)S(1)} custom-call(f32[128,128]{1,0:T(8,128)S(1)} %cholesky.211), custom_call_target="Cholesky" | custom-call | tf_op jit(solution)/shard_map/jit(cholesky)/cholesky | solution.py:34
  156.0 0.6 select_reduce_fusion
  156.6 1.3 fusion.27
  158.2 0.7 copy-done.2
  159.7 0.7 convolution_add_fusion.1
  160.5 11.9 %cholesky.136 = f32[128,128]{1,0:T(8,128)S(1)} custom-call(f32[128,128]{1,0:T(8,128)S(1)} %cholesky.208), custom_call_target="Cholesky" | custom-call | tf_op jit(solution)/shard_map/jit(cholesky)/cholesky | solution.py:34
  172.5 10.6 %custom-call.15 = f32[1,128,128]{1,2,0:T(8,128)S(1)} custom-call(f32[1,128,128]{2,1,0:T(8,128)} %get-tuple-element.50), custom_call_target="InvertDiagBlocksLowerTriangular" | custom-call | tf_op jit(solution)/shard_map/jit(cholesky)/cholesky | solution.py:34
  183.1 0.9 constant_dynamic-update-slice_fusion.1
  184.0 0.9 convolution_subtract_fusion.6
  184.9 2.9 %cholesky.194 = f32[32,32]{1,0:T(8,128)S(1)} custom-call(f32[32,32]{1,0:T(8,128)S(1)} %convolution_subtract_fusion.6), custom_call_target="Cholesky" | custom-call | tf_op jit(solution)/shard_map/jit(cholesky)/cholesky | solution.py:34
  187.8 0.6 compare_reduce_fusion
  188.5 0.6 compare_reduce_fusion.1
  190.4 9.8 %custom-call.13 = f32[1,128,128]{1,2,0:T(8,128)S(1)} custom-call(f32[1,128,128]{2,1,0:T(8,128)S(1)} %get-tuple-element.48), custom_call_target="InvertDiagBlocksLowerTriangular" | custom-call | tf_op jit(solution)/shard_map/jit(cholesky)/cholesky | solution.py:34
  200.5 2.9 %cholesky.156 = f32[32,32]{1,0:T(8,128)S(1)} custom-call(f32[32,32]{1,0:T(8,128)S(1)} %convolution_subtract_fusion.7), custom_call_target="Cholesky" | custom-call | tf_op jit(solution)/shard_map/jit(cholesky)/cholesky | solution.py:34
  203.5 0.6 compare_reduce_fusion.2
  204.1 0.6 compare_reduce_fusion.3
  206.1 0.7 pad_maximum_fusion.6
  206.8 19.7 %custom-call.14 = f32[2,128,128]{1,2,0:T(8,128)S(1)} custom-call(f32[2,128,128]{2,1,0:T(8,128)S(1)} %get-tuple-element.63), custom_call_target="InvertDiagBlocksLowerTriangular" | custom-call | tf_op jit(solution)/shard_map/triangular_solve/custom-call.0 | solution.py:35
  226.4 0.6 fusion.15
  228.8 20.5 %custom-call.16 = f32[2,128,128]{1,2,0:T(8,128)S(1)} custom-call(f32[2,128,128]{2,1,0:T(8,128)} %get-tuple-element.64), custom_call_target="InvertDiagBlocksLowerTriangular" | custom-call | tf_op jit(solution)/shard_map/triangular_solve/custom-call.0 | solution.py:35
  249.3 0.6 fusion.13
  251.8 0.8 copy-done.3
  253.1 0.5 fusion.22
  254.1 0.5 fusion.21
  255.7 1.1 maximum_bitcast_fusion.1
  256.8 1.1 maximum_bitcast_fusion
  (82 shorter events, 9.8 us)
Async XLA Ops:
  7.2 71.8 %all-gather.2.cloned.1.call-start = ((), (), s32[]{:S(2)}) async-start(), calls=%async_computation.1 | async-start | bytes 2621440 | tf_op jit(solution)/shard_map/all_gather | solution.py:59
  8.6 8.5 %copy-start.13 = (s32[2,1,1]{0,2,1:T(1,128)S(1)}, s32[2,1,1]{0,2,1:T(1,128)}, u32[]{:S(2)}) copy-start(s32[2,1,1]{0,2,1:T(1,128)} %param.17) | copy-start | bytes 28
  8.6 11.0 %copy-start.6 = (bf16[2,1,1,1024,160]{3,4,2,1,0:T(8,128)(2,1)S(1)}, bf16[2,1,1,1024,160]{3,4,2,1,0:T(8,128)(2,1)}, u32[]{:S(2)}) copy-start(bf16[2,1,1,1024,160]{3,4,2,1,0:T(8,128)(2,1)} %param.16) | copy-start | bytes 1966084
  8.6 11.0 %copy-start.14 = (bf16[2,1,1,1024,160]{3,4,2,1,0:T(8,128)(2,1)S(1)}, bf16[2,1,1,1024,160]{3,4,2,1,0:T(8,128)(2,1)}, u32[]{:S(2)}) copy-start(bf16[2,1,1,1024,160]{3,4,2,1,0:T(8,128)(2,1)} %param.18) | copy-start | bytes 1966084
  10.7 58.8 %all-to-all-start = ((bf16[4,2,1,256,160]{3,4,2,1,0:T(8,128)(2,1)}), bf16[4,2,1,256,160]{3,4,2,1,0:T(8,128)(2,1)S(1)}, u32[]{:S(2)}, u32[]{:S(2)}) async-start(bf16[4,2,1,256,160]{3,4,2,1,0:T(8,128)(2,1)} %stack.25), calls=%async_computation | async-start | bytes 1310720 | tf_op jit(solution)/shard_map/all_to_all | solution.py:55
  17.1 122.9 %all-reduce.6.cloned.1.call-start = ((), (), s32[]{:S(2)}) async-start(), calls=%async_computation.2 | async-start | bytes 2621440 | tf_op jit(solution)/shard_map/psum | solution.py:10
  81.4 1.5 copy-start.4
  84.0 56.0 %copy-start.15 = (bf16[2,1,1,1024,160]{3,4,2,1,0:T(8,128)(2,1)S(1)}, bf16[2,1,1,1024,160]{3,4,2,1,0:T(8,128)(2,1)}, u32[]{:S(2)}) copy-start(bf16[2,1,1,1024,160]{3,4,2,1,0:T(8,128)(2,1)} %param.18) | copy-start | bytes 1966084
  142.6 1.5 copy-start
  143.4 13.3 %copy-start.10 = (bf16[1024,160]{0,1:T(8,128)(2,1)S(1)}, bf16[1024,160]{0,1:T(8,128)(2,1)}, u32[]{:S(2)}) copy-start(bf16[1024,160]{0,1:T(8,128)(2,1)} %get-tuple-element.39) | copy-start | bytes 983044
  144.2 13.8 %copy-start.12 = (bf16[1024,160]{0,1:T(8,128)(2,1)S(1)}, bf16[1024,160]{0,1:T(8,128)(2,1)}, u32[]{:S(2)}) copy-start(bf16[1024,160]{0,1:T(8,128)(2,1)} %get-tuple-element.38) | copy-start | bytes 983044
  144.2 15.0 %copy-start.8 = (f32[160,160]{1,0:T(8,128)}, f32[160,160]{1,0:T(8,128)S(1)}, u32[]{:S(2)}) copy-start(f32[160,160]{1,0:T(8,128)S(1)} %fusion.47) | copy-start | bytes 307204
  158.2 0.7 copy-start.2
  227.1 1.2 copy-start.5
  251.6 0.9 copy-start.3
  251.7 1.4 copy-start.7
  251.7 1.9 copy-start.1
  253.1 1.6 copy-start.11
  254.1 1.0 copy-start.9
Sparse Core Ops, SparseCore 0:
  9.5 69.3 all-gather.1
  82.9 57.0 all-reduce.5
